TPU v7x, 512 devices: a whole 4x8x8 slice. The times are simulated.
512 devices in a mesh: grp: 16 (over y, x_lo), blk: 32 (over z, x_hi, core).
Axes of the slice: x: 4 (x_hi: 2, x_lo: 2; x = x_hi * 2 + x_lo), y: 8, z: 8, core: 2. Of those that a mesh axis runs over, the one named last changes fastest.
Arguments:
- amplitudes: float32 [128, 128, 2048], P('blk', None, 'grp'), may hold values from -6 to 6
- ladder_ints: float32 [2048, 2048], P('grp', 'blk'), may hold values from -0.375 to 0.375
- cycle_ints: float32 [2048, 2048], P('grp', 'blk'), may hold values from -0.375 to 0.375
- occ_coupling: float32 [128, 128], replicated, may hold values from -1.5 to 1.5
- occ_irrep: int32 [128], replicated, may hold values from 0 to 7
- pair_irrep: int32 [16], replicated, may hold values from 0 to 7
- screen: int32 [16, 16], replicated, may hold values 0 or 1
- block_order: int32 [16], replicated, may hold values from 0 to 15, each once
Outputs:
- residual: float32 [128, 128, 2048], P('blk', None, 'grp')
Inputs may be any that keep to these rules, and one draw needn't show every extreme that they name: block_order names every block once.
All inputs are finite; a program needn't handle non-finite values.
Results may differ from a plain program's by a relative error of at most 0.000071.
Values sent between devices are 32-bit elements; how exact they have to be, the bound alone decides.
A program may use at most 64 MiB of HBM per device.

v0:
```python
import jax
import jax.numpy as jnp
from jax import lax
from jax.sharding import PartitionSpec as P


def shards(
    amplitudes, ladder_ints, cycle_ints, occ_coupling, occ_irrep, pair_irrep, screen, block_order
):
    highest = lax.Precision.HIGHEST
    rows_i, occ, cols_g = amplitudes.shape
    nblocks = pair_irrep.shape[0]
    blk_grp = nblocks // lax.axis_size("grp")
    tile = cols_g // blk_grp
    grp_id = lax.axis_index("grp")
    row_id = lax.axis_index("blk")
    my_occ = lax.dynamic_slice_in_dim(occ_irrep, row_id * rows_i, rows_i)
    my_labels = lax.dynamic_slice_in_dim(pair_irrep, grp_id * blk_grp, blk_grp)
    my_screen = lax.dynamic_slice_in_dim(screen, grp_id * blk_grp, blk_grp, 0).astype(jnp.float32)
    pair_sym = jnp.bitwise_xor(my_occ[:, None], occ_irrep[None, :])
    amp_mask = (pair_sym[:, :, None] == my_labels[None, None, :]).astype(jnp.float32)
    amps3 = (amplitudes.reshape(rows_i, occ, blk_grp, tile) * amp_mask[:, :, :, None]).reshape(
        rows_i, occ, cols_g
    )
    amps = amps3.reshape(rows_i * occ, cols_g)
    coupling = occ_coupling * (occ_irrep[:, None] == occ_irrep[None, :]).astype(jnp.float32)
    label_cols = pair_irrep.astype(jnp.float32)[None, :]
    mine_rows = my_labels.astype(jnp.float32)[:, None]
    local_panels = jnp.stack((ladder_ints, cycle_ints))
    piece = lax.all_gather(local_panels, "blk", axis=2, tiled=True)
    count = piece.shape[2]
    col_blk = jnp.arange(count, dtype=jnp.int32) // tile
    onehot = (col_blk[None, :] == jnp.arange(nblocks, dtype=jnp.int32)[:, None]).astype(jnp.float32)
    col_lab = jnp.dot(label_cols, onehot, precision=highest)
    same = (mine_rows == col_lab).astype(jnp.float32)
    kept = jnp.dot(my_screen, onehot, precision=highest)
    keep_ladder = same * kept
    ladder_panel = (piece[0].reshape(blk_grp, tile, count) * keep_ladder[:, None, :]).reshape(
        cols_g, count
    )
    cycle_panel = (piece[1].reshape(blk_grp, tile, count) * same[:, None, :]).reshape(cols_g, count)
    ladder = jnp.dot(amps, ladder_panel, precision=highest, preferred_element_type=jnp.float32)
    inner = jnp.dot(amps, cycle_panel, precision=highest, preferred_element_type=jnp.float32)
    cycle = jnp.einsum(
        "ikx,kj->ijx", inner.reshape(rows_i, occ, count), coupling, precision=highest
    )
    partial_value = ladder + cycle.reshape(rows_i * occ, count)
    ordered = jnp.take(partial_value.reshape(rows_i, occ, nblocks, tile), block_order, axis=2)
    ordered = ordered.reshape(rows_i, occ, nblocks * tile)
    moved = lax.all_to_all(ordered, "blk", split_axis=1, concat_axis=0, tiled=True)
    anti = ordered - jnp.transpose(moved, (1, 0, 2))
    result = lax.psum_scatter(anti, "grp", scatter_dimension=2, tiled=True)
    return result


def solution(mesh):
    placed = (P("blk", None, "grp"), P("grp", "blk"), P("grp", "blk"), P(), P(), P(), P(), P())
    return jax.shard_map(
        shards, mesh=mesh, in_specs=placed, out_specs=P("blk", None, "grp"), check_vma=False
    )
```

profile of v0, /device:TPU:18, one launch (start us, length us, event | category | flops | bytes accessed | tf_op | source)
XLA Modules:
  0.0 363.0 jit_solution(6302833797781969086)
XLA Ops:
  6.5 1.4 pad_maximum_fusion
  8.1 1.3 dynamic_slice.10
  10.1 0.9 fusion.8
  10.9 0.8 fusion.9
  11.8 0.7 dynamic_slice.9
  13.2 0.7 compare_and_fusion
  13.9 1.4 fusion.22
  15.3 1.1 broadcast_multiply_fusion
  16.4 84.0 %all-gather.2.cloned.1.call-done = f32[2,128,2048]{1,2,0:T(8,128)} async-done(((f32[2,128,64]{1,2,0:T(8,128)}), f32[2,128,2048]{1,2,0:T(8,128)}) %all-gather.2.cloned.1.call-update) | async-done | bytes 2097168 | tf_op jit(solution)/shard_map/all_gather | solution.py:30
  100.4 4.8 %fusion.2 = f32[4,128,2048]{2,1,0:T(8,128)S(1)} fusion(f32[4,128,128]{2,1,0:T(8,128)S(1)} %broadcast_multiply_fusion, f32[2,128,2048]{1,2,0:T(8,128)} %all-gather.2.cloned.1.call-done, f32[2048]{0:T(1024)S(1)} %convert_element_type.28), kind=kOutput, calls=%fused_computation.7 | convolution fusion | flops 1610874880 | bytes 5513216 | tf_op jit(solution)/shard_map/dot_general | solution.py:43
  105.3 4.1 %fusion.10 = f32[128,4,2048]{2,0,1:T(8,128)S(1)} fusion(f32[4,128,2048]{2,1,0:T(8,128)S(1)} %fusion.2, f32[128,128]{1,0:T(8,128)S(1)} %copy-done.1, s32[128]{0:T(128)S(1)} %copy-done.2), kind=kOutput, calls=%fused_computation.17 | convolution fusion | flops 1610645504 | bytes 8454656 | tf_op jit(solution)/shard_map/ikx,kj->ijx/dot_general | solution.py:44
  109.4 3.6 %fusion = f32[64,8,16,128]{3,1,2,0:T(8,128)S(1)} fusion(f32[128,4,2048]{2,0,1:T(8,128)S(1)} %fusion.10, f32[512,128]{1,0:T(8,128)S(1)} %bitcast.55, f32[2,128,2048]{1,2,0:T(8,128)S(1)} %copy-done, f32[2048]{0:T(1024)S(1)} %get-tuple-element.5), kind=kOutput, calls=%fused_computation.4 | convolution fusion | flops 1611923456 | bytes 9707520 | tf_op jit(solution)/shard_map/dot_general | solution.py:42
  113.0 1.1 copy.40
  114.2 3.2 copy.30
  117.4 5.0 %gather_fusion = f32[16,4,128,128]{3,2,1,0:T(8,128)} fusion(f32[4,128,16,128]{3,1,2,0:T(8,128)} %copy.30, s32[1024]{0:T(1024)S(1)} %pad_clamp_fusion), kind=kCustom, calls=%fused_computation | custom fusion | bytes 8388672 | tf_op jit(solution)/shard_map/jit(_take)/gather | solution.py:48
  122.4 5.3 %copy.31 = f32[4,128,16,128]{1,3,2,0:T(8,128)} copy(f32[4,128,16,128]{3,1,0,2:T(8,128)} %bitcast.51) | data formatting | bytes 8388608 | tf_op jit(solution)/shard_map/jit(_take)/gather | solution.py:48
  127.7 3.8 %bitcast_select_fusion = f32[4,128,2048]{1,2,0:T(8,128)} fusion(f32[4,128,16,128]{1,3,2,0:T(8,128)} %copy.31, pred[2048]{0:T(1024)(128)(4,1)S(1)} %broadcast_bitcast_fusion), kind=kLoop, calls=%fused_computation.3 | loop fusion | flops 1048576 | bytes 8390656 | tf_op jit(solution)/shard_map/jit(_take)/select_n | solution.py:48
  131.5 5.5 %copy.32 = f32[4,128,2048]{2,0,1:T(4,128)} copy(f32[4,128,2048]{1,2,0:T(8,128)} %bitcast_select_fusion) | data formatting | bytes 8388608 | tf_op jit(solution)/shard_map/jit(_take)/select_n | solution.py:48
  137.0 101.9 %all_to_all.18 = f32[4,128,2048]{2,0,1:T(4,128)S(1)} all-to-all(f32[4,128,2048]{2,0,1:T(4,128)} %copy.32), channel_id=1, replica_groups=mesh['grp'=16,'blk'=32] {'blk'}, dimensions={1} | all-to-all | bytes 8388608 | tf_op jit(solution)/shard_map/all_to_all | solution.py:50
  238.9 5.5 %copy.33 = f32[32,4,4,2048]{3,2,1,0:T(4,128)} copy(f32[32,4,4,2048]{3,1,2,0:T(4,128)S(1)} %bitcast.53) | data formatting | bytes 8388608 | tf_op jit(solution)/shard_map/all_to_all | solution.py:50
  244.5 5.3 %copy.34 = f32[128,4,2048]{0,2,1:T(8,128)} copy(f32[128,4,2048]{2,1,0:T(4,128)} %bitcast.54) | data formatting | bytes 8388608 | tf_op jit(solution)/shard_map/all_to_all | solution.py:50
  249.8 5.1 %bitcast_subtract_fusion = f32[4,128,2048]{1,2,0:T(8,128)} fusion(f32[128,4,2048]{0,2,1:T(8,128)} %copy.34, f32[4,128,16,128]{1,3,2,0:T(8,128)} %copy.31, pred[2048]{0:T(1024)(128)(4,1)S(1)} %broadcast_bitcast_fusion), kind=kLoop, calls=%fused_computation.2 | loop fusion | flops 2097152 | bytes 12584960 | tf_op jit(solution)/shard_map/sub | solution.py:51
  254.8 99.5 %reduce-scatter.2.cloned.1.call-done = f32[4,128,128]{1,2,0:T(8,128)} async-done(((f32[4,128,2048]{1,2,0:T(8,128)}), f32[4,128,128]{1,2,0:T(8,128)}) %reduce-scatter.2.cloned.1.call-update) | async-done | bytes 262160 | tf_op jit(solution)/shard_map/reduce_scatter | solution.py:52
  354.3 1.8 copy.35
  (16 shorter events, 0.8 us)
Async XLA Ops:
  6.5 98.7 %copy-start.2 = (s32[128]{0:T(128)S(1)}, s32[128]{0:T(128)}, u32[]{:S(2)}) copy-start(s32[128]{0:T(128)} %param.12) | copy-start | bytes 1540
  6.5 98.7 %copy-start.1 = (f32[128,128]{1,0:T(8,128)S(1)}, f32[128,128]{1,0:T(8,128)}, u32[]{:S(2)}) copy-start(f32[128,128]{1,0:T(8,128)} %param.11) | copy-start | bytes 196612
  6.5 93.9 %all-gather.2.cloned.1.call-start = ((), (), s32[]{:S(2)}) async-start(), calls=%async_computation.2 | async-start | bytes 2162688 | tf_op jit(solution)/shard_map/all_gather | solution.py:30
  8.0 346.3 %reduce-scatter.2.cloned.1.call-start = ((), (), s32[]{:S(2)}) async-start(), calls=%async_computation.3 | async-start | bytes 4456448 | tf_op jit(solution)/shard_map/reduce_scatter | solution.py:52
  105.3 4.1 %copy-start = (f32[2,128,2048]{1,2,0:T(8,128)S(1)}, f32[2,128,2048]{1,2,0:T(8,128)}, u32[]{:S(2)}) copy-start(f32[2,128,2048]{1,2,0:T(8,128)} %all-gather.2.cloned.1.call-done) | copy-start | bytes 6291460
Sparse Core Ops, SparseCore 0:
  10.8 89.6 all-gather.1
  255.0 99.3 reduce-scatter.1
where the time goes:
time: 364 us; the launch traced here: 363 us
  waiting for transfers between devices  184 us (51%)
  blocking collectives  102 us (28%)
  local copies, waits for them, and re-layouts  34.9 us (10%)
  matrix products  14.2 us (4%)
  between operations  14.2 us (4%)
  other arithmetic  14.1 us (4%)
    all_to_all x1, blocking collectives, shards(): lax.all_to_all(ordered, 'blk', split_axis=1, concat_axis=0, tiled=True)  102 us
    reduce_scatter x1, waiting for transfers between devices, shards(): result = lax.psum_scatter(anti, 'grp', scatter_dimension=2, tiled=True)  99.5 us
    all_gather x1, waiting for transfers between devices, shards(): piece = lax.all_gather(local_panels, 'blk', axis=2, tiled=True)  84 us
    all_to_all x2, local copies, waits for them, and re-layouts, shards(): lax.all_to_all(ordered, 'blk', split_axis=1, concat_axis=0, tiled=True)  10.8 us
    gather x2, local copies, waits for them, and re-layouts, shards(): jnp.take(partial_value.reshape(rows_i, occ, nblocks, tile), block_order,...  10.3 us
  transfers between devices with their start and end apart: 2, of which 2 were waited for; matrix products, arithmetic and copies ran while one was open for 2% of the time, Pallas kernels for 0%

commit v1 on v0

--- a/solution.py
+++ b/solution.py
@@ -27,7 +27,16 @@
     label_cols = pair_irrep.astype(jnp.float32)[None, :]
     mine_rows = my_labels.astype(jnp.float32)[:, None]
     local_panels = jnp.stack((ladder_ints, cycle_ints))
-    piece = lax.all_gather(local_panels, "blk", axis=2, tiled=True)
+    block_mark = lambda original, comm_axis: jnp.concatenate(
+        lax.all_to_all(
+            jnp.stack([original for _ in range(lax.axis_size(comm_axis))], axis=0),
+            axis_name=comm_axis,
+            split_axis=0,
+            concat_axis=0,
+        ),
+        axis=2,
+    )
+    piece = block_mark(local_panels, "blk")
     count = piece.shape[2]
     col_blk = jnp.arange(count, dtype=jnp.int32) // tile
     onehot = (col_blk[None, :] == jnp.arange(nblocks, dtype=jnp.int32)[:, None]).astype(jnp.float32)

time: 364 us -> 335 us (0.920)
  waiting for transfers between devices: 184 us -> 147 us
  starting transfers between devices: 0.04 us -> 12.3 us
    all_gather x1 -> x0, waiting for transfers between devices: 84 us -> none  [shards(): piece = lax.all_gather(local_panels, 'blk', axis=2, tiled=True)]
    all_to_all x0 -> x1, waiting for transfers between devices: none -> 46.8 us  [shards(): lax.all_to_all(jnp.stack([original for _ in range(lax.axis_size(comm_axis...]
    all_to_all x0 -> x1, starting transfers between devices: none -> 12.3 us  [shards(): lax.all_to_all(jnp.stack([original for _ in range(lax.axis_size(comm_axis...]
  transfers between devices with their start and end apart: 2 -> 2, of which waited for: 2 -> 2; matrix products, arithmetic and copies ran while one was open for 2% -> 1% of each run, Pallas kernels for 0% -> 0%
where the time goes in v1:
time: 335 us
  waiting for transfers between devices  147 us (44%)
  blocking collectives  103 us (31%)
  local copies, waits for them, and re-layouts  35.5 us (11%)
  between operations  14.2 us (4%)
  starting transfers between devices  12.3 us (4%)
  matrix products  12.2 us (4%)
  other arithmetic  11.3 us (3%)
    all_to_all x1, blocking collectives, shards(): lax.all_to_all(ordered, 'blk', split_axis=1, concat_axis=0, tiled=True)  103 us
    reduce_scatter x1, waiting for transfers between devices, shards(): result = lax.psum_scatter(anti, 'grp', scatter_dimension=2, tiled=True)  99.9 us
    all_to_all x1, waiting for transfers between devices, shards(): lax.all_to_all(jnp.stack([original for _ in range(lax.axis_size(comm_axis...  46.8 us
    all_to_all x1, starting transfers between devices, shards(): lax.all_to_all(jnp.stack([original for _ in range(lax.axis_size(comm_axis...  12.3 us
    all_to_all x2, local copies, waits for them, and re-layouts, shards(): lax.all_to_all(ordered, 'blk', split_axis=1, concat_axis=0, tiled=True)  10.8 us
    gather x2, local copies, waits for them, and re-layouts, shards(): jnp.take(partial_value.reshape(rows_i, occ, nblocks, tile), block_order,...  10.3 us
  transfers between devices with their start and end apart: 2, of which 2 were waited for; matrix products, arithmetic and copies ran while one was open for 1% of the time, Pallas kernels for 0%

profile of v1, /device:TPU:18, one launch (start us, length us, event | category | flops | bytes accessed | tf_op | source)
XLA Modules:
  0.0 334.7 jit_solution(8411419126447753994)
XLA Ops:
  6.5 0.8 pad_maximum_fusion
  7.4 1.6 stack.11
  9.0 12.3 %all-to-all-start = ((f32[32,2,128,64]{2,3,1,0:T(8,128)}), f32[32,2,128,64]{2,3,1,0:T(8,128)S(1)}, u32[]{:S(2)}, u32[]{:S(2)}) async-start(f32[32,2,128,64]{2,3,1,0:T(8,128)} %stack.11), calls=%async_computation | async-start | bytes 4194304 | tf_op jit(solution)/shard_map/all_to_all | solution.py:31
  21.3 0.6 dynamic_slice.10
  22.6 0.9 fusion.1
  23.9 0.7 fusion.15
  24.8 46.8 %all-to-all-done = f32[32,2,128,64]{2,3,1,0:T(8,128)S(1)} async-done(((f32[32,2,128,64]{2,3,1,0:T(8,128)}), f32[32,2,128,64]{2,3,1,0:T(8,128)S(1)}, u32[]{:S(2)}, u32[]{:S(2)}) %all-to-all-start) | async-done | bytes 2097184 | tf_op jit(solution)/shard_map/all_to_all | solution.py:31
  71.6 0.2 copy.44
  71.8 0.7 slice_multiply_fusion.1
  72.5 3.5 %fusion.19 = f32[4,128,2048]{2,1,0:T(8,128)S(1)} fusion(f32[4,128,128]{2,1,0:T(8,128)S(1)} %broadcast_multiply_fusion, f32[128,2048,1]{0,1,2:T(8,128)S(1)} %bitcast.58), kind=kOutput, calls=%fused_computation.42 | convolution fusion | flops 1610612736 | bytes 5505024 | tf_op jit(solution)/shard_map/dot_general | solution.py:52
  76.1 4.1 %fusion.3 = f32[128,4,2048]{2,0,1:T(8,128)S(1)} fusion(f32[4,128,2048]{2,1,0:T(8,128)S(1)} %fusion.19, f32[128,128]{1,0:T(8,128)S(1)} %copy-done.1, s32[128]{0:T(128)S(1)} %copy-done.2), kind=kOutput, calls=%fused_computation.13 | convolution fusion | flops 1610645504 | bytes 8454656 | tf_op jit(solution)/shard_map/ikx,kj->ijx/dot_general | solution.py:53
  80.2 3.6 %fusion = f32[64,8,16,128]{3,1,2,0:T(8,128)S(1)} fusion(f32[128,4,2048]{2,0,1:T(8,128)S(1)} %fusion.3, f32[512,128]{1,0:T(8,128)S(1)} %bitcast.59, f32[128,2048]{0,1:T(8,128)S(1)} %bitcast.57), kind=kOutput, calls=%fused_computation.4 | convolution fusion | flops 1611661312 | bytes 9699328 | tf_op jit(solution)/shard_map/dot_general | solution.py:51
  83.7 0.9 copy.42
  84.6 3.4 %copy.32 = f32[4,128,16,128]{3,1,2,0:T(8,128)} copy(f32[4,128,16,128]{3,2,1,0:T(8,128)S(1)} %bitcast.53) | data formatting | bytes 8388608 | tf_op jit(solution)/shard_map/reshape | solution.py:57
  88.1 5.0 %gather_fusion = f32[16,4,128,128]{3,2,1,0:T(8,128)} fusion(f32[4,128,16,128]{3,1,2,0:T(8,128)} %copy.32, s32[1024]{0:T(1024)S(1)} %pad_clamp_fusion), kind=kCustom, calls=%fused_computation | custom fusion | bytes 8388672 | tf_op jit(solution)/shard_map/jit(_take)/gather | solution.py:57
  93.0 5.3 %copy.33 = f32[4,128,16,128]{1,3,2,0:T(8,128)} copy(f32[4,128,16,128]{3,1,0,2:T(8,128)} %bitcast.52) | data formatting | bytes 8388608 | tf_op jit(solution)/shard_map/jit(_take)/gather | solution.py:57
  98.4 3.8 %bitcast_select_fusion = f32[4,128,2048]{1,2,0:T(8,128)} fusion(f32[4,128,16,128]{1,3,2,0:T(8,128)} %copy.33, pred[2048]{0:T(1024)(128)(4,1)S(1)} %broadcast_bitcast_fusion), kind=kLoop, calls=%fused_computation.3 | loop fusion | flops 1048576 | bytes 8390656 | tf_op jit(solution)/shard_map/jit(_take)/select_n | solution.py:57
  102.2 5.5 %copy.34 = f32[4,128,2048]{2,0,1:T(4,128)} copy(f32[4,128,2048]{1,2,0:T(8,128)} %bitcast_select_fusion) | data formatting | bytes 8388608 | tf_op jit(solution)/shard_map/jit(_take)/select_n | solution.py:57
  107.7 102.6 %all_to_all.23 = f32[4,128,2048]{2,0,1:T(4,128)S(1)} all-to-all(f32[4,128,2048]{2,0,1:T(4,128)} %copy.34), channel_id=1, replica_groups=mesh['grp'=16,'blk'=32] {'blk'}, dimensions={1} | all-to-all | bytes 8388608 | tf_op jit(solution)/shard_map/all_to_all | solution.py:59
  210.3 5.5 %copy.35 = f32[32,4,4,2048]{3,2,1,0:T(4,128)} copy(f32[32,4,4,2048]{3,1,2,0:T(4,128)S(1)} %bitcast.54) | data formatting | bytes 8388608 | tf_op jit(solution)/shard_map/all_to_all | solution.py:59
  215.8 5.3 %copy.36 = f32[128,4,2048]{0,2,1:T(8,128)} copy(f32[128,4,2048]{2,1,0:T(4,128)} %bitcast.55) | data formatting | bytes 8388608 | tf_op jit(solution)/shard_map/all_to_all | solution.py:59
  221.1 5.0 %bitcast_subtract_fusion = f32[4,128,2048]{1,2,0:T(8,128)} fusion(f32[128,4,2048]{0,2,1:T(8,128)} %copy.36, f32[4,128,16,128]{1,3,2,0:T(8,128)} %copy.33, pred[2048]{0:T(1024)(128)(4,1)S(1)} %broadcast_bitcast_fusion), kind=kLoop, calls=%fused_computation.2 | loop fusion | flops 2097152 | bytes 12584960 | tf_op jit(solution)/shard_map/sub | solution.py:60
  226.1 99.9 %reduce-scatter.2.cloned.1.call-done = f32[4,128,128]{1,2,0:T(8,128)} async-done(((f32[4,128,2048]{1,2,0:T(8,128)}), f32[4,128,128]{1,2,0:T(8,128)}) %reduce-scatter.2.cloned.1.call-update) | async-done | bytes 262160 | tf_op jit(solution)/shard_map/reduce_scatter | solution.py:61
  326.1 1.8 copy.37
  (24 shorter events, 0.7 us)
Async XLA Ops:
  6.5 14.8 %copy-start.3 = (s32[16]{0:T(128)S(1)}, s32[16]{0:T(128)}, u32[]{:S(2)}) copy-start(s32[16]{0:T(128)} %param.13) | copy-start | bytes 196
  6.5 17.2 %copy-start.2 = (s32[128]{0:T(128)S(1)}, s32[128]{0:T(128)}, u32[]{:S(2)}) copy-start(s32[128]{0:T(128)} %param.12) | copy-start | bytes 1540
  6.5 17.3 %copy-start.4 = (s32[16]{0:T(128)S(1)}, s32[16]{0:T(128)}, u32[]{:S(2)}) copy-start(s32[16]{0:T(128)} %param.15) | copy-start | bytes 196
  6.5 18.1 %copy-start = (f32[4,128,128]{2,1,0:T(8,128)S(1)}, f32[4,128,128]{2,1,0:T(8,128)}, u32[]{:S(2)}) copy-start(f32[4,128,128]{2,1,0:T(8,128)} %param.8) | copy-start | bytes 786436
  9.0 62.6 %all-to-all-start = ((f32[32,2,128,64]{2,3,1,0:T(8,128)}), f32[32,2,128,64]{2,3,1,0:T(8,128)S(1)}, u32[]{:S(2)}, u32[]{:S(2)}) async-start(f32[32,2,128,64]{2,3,1,0:T(8,128)} %stack.11), calls=%async_computation | async-start | bytes 4194304 | tf_op jit(solution)/shard_map/all_to_all | solution.py:31
  21.2 304.8 %reduce-scatter.2.cloned.1.call-start = ((), (), s32[]{:S(2)}) async-start(), calls=%async_computation.3 | async-start | bytes 4456448 | tf_op jit(solution)/shard_map/reduce_scatter | solution.py:61
  71.8 4.2 %copy-start.1 = (f32[128,128]{1,0:T(8,128)S(1)}, f32[128,128]{1,0:T(8,128)}, u32[]{:S(2)}) copy-start(f32[128,128]{1,0:T(8,128)} %param.11) | copy-start | bytes 196612
Sparse Core Ops, SparseCore 0:
  226.3 99.7 reduce-scatter.1
